TPU v7x, 256 devices: a whole 4x4x8 slice. The times are simulated.
256 devices in a mesh: view: 32 (over y, x, core), strip: 8 (over z).
Axes of the slice: x: 4, y: 4, z: 8, core: 2. Of those that a mesh axis runs over, the one named last changes fastest.
Arguments:
- tokens: bfloat16 [32, 1024, 1536], P('view', 'strip'), may hold values from -48 to 48
- source_ids: int32 [32, 8, 5], replicated, may hold values from 0 to 255, as said below
- source_count: int32 [32, 8], replicated, may hold values from 2 to 5, as said below
- self_query: bfloat16 [1536, 1536], P(None, 'strip'), may hold values from -24 to 24
- self_key: bfloat16 [1536, 1536], P(None, 'strip'), may hold values from -24 to 24
- self_value: bfloat16 [1536, 1536], P(None, 'strip'), may hold values from -0.15625 to 0.15625
- self_out: bfloat16 [1536, 1536], P('strip'), may hold values from -1.1953125 to 1.1953125
- cross_query: bfloat16 [1536, 1536], P(None, 'strip'), may hold values from -24 to 24
- cross_key: bfloat16 [1536, 1536], P(None, 'strip'), may hold values from -24 to 24
- cross_value: bfloat16 [1536, 1536], P(None, 'strip'), may hold values from -0.15625 to 0.15625
- cross_out: bfloat16 [1536, 1536], P('strip'), may hold values from -1.1953125 to 1.1953125
- mlp_up: bfloat16 [1536, 6144], P(None, 'strip'), may hold values from -0.15625 to 0.15625
- mlp_down: bfloat16 [6144, 1536], P('strip'), may hold values from -0.078125 to 0.078125
Outputs:
- mixed: bfloat16 [32, 1024, 1536], P('view', 'strip')
Inputs may be any that keep to these rules, and one draw needn't show every extreme that they name: `source_ids`: entry k of strip s of view v names a strip of another view than v; entries with k >= source_count[v, s] are unused. Among all 40 entries of one destination view, used or not, each other view is named at most 2 times, and some view exactly 2 times. `source_count`: every view has a strip with all 5 entries in use.
All inputs are finite; a program needn't handle non-finite values.
Results may differ from a plain program's by a relative error of at most 0.015.
Values may be sent and summed in bfloat16 or wider, within the bound.
No kernel may reach another device: no remote copies, remote signals or barrier semaphores. Data moves between devices by JAX's collectives and lax.ppermute only.
A program may use at most 128 MiB of HBM per device.

v0:
```python
import math
import jax
import jax.numpy as jnp
from jax import lax
from jax.sharding import PartitionSpec as P

HEAD_DIM = 64
SLOTS = 5


def rms_rows(values_in):
    widened = values_in.astype(jnp.float32)
    scaled = widened * lax.rsqrt(jnp.mean(widened * widened, axis=-1, keepdims=True) + 1e-06)
    return scaled.astype(jnp.bfloat16)


def attend_heads(query_heads, key_heads, value_heads, key_mask):
    scale = 1.0 / math.sqrt(HEAD_DIM)
    scores = (
        jnp.einsum("qhe,khe->hqk", query_heads, key_heads, preferred_element_type=jnp.float32)
        * scale
    )
    scores = jnp.where(key_mask[None, None, :], scores, -1e30)
    weights = jax.nn.softmax(scores, axis=-1).astype(jnp.bfloat16)
    mixed_heads = jnp.einsum(
        "hqk,khe->qhe", weights, value_heads, preferred_element_type=jnp.float32
    )
    return mixed_heads.reshape(mixed_heads.shape[0], -1).astype(jnp.bfloat16)


def branch_term(mixed_rows, weight):
    return jnp.dot(mixed_rows, weight, preferred_element_type=jnp.float32)


def per_device(
    tokens,
    source_ids,
    source_count,
    self_query,
    self_key,
    self_value,
    self_out,
    cross_query,
    cross_key,
    cross_value,
    cross_out,
    mlp_up,
    mlp_down,
):
    n_view = lax.axis_size("view")
    n_strip = lax.axis_size("strip")
    my_view = lax.axis_index("view")
    strip_rows = tokens.shape[1]
    head_cols = self_query.shape[1]
    heads_here = head_cols // HEAD_DIM
    capacity = (n_strip * SLOTS + n_view - 2) // (n_view - 1)
    normed = rms_rows(tokens[0])
    stacked = jnp.concatenate(
        [self_query, self_key, self_value, cross_query, cross_key, cross_value, mlp_up], 1
    )
    split_at = 6 * head_cols
    product = jnp.dot(
        lax.all_gather(normed, "strip", axis=0, tiled=True),
        stacked,
        preferred_element_type=jnp.float32,
    )
    projected = jnp.concatenate(
        [product[:, :split_at], jax.nn.gelu(product[:, split_at:])], 1
    ).astype(jnp.bfloat16)
    total_rows = projected.shape[0]
    flat_ids = source_ids.reshape(n_view, -1)
    source_view = flat_ids // n_strip
    source_strip = flat_ids % n_strip
    entry_count = flat_ids.shape[1]
    entry_order = jnp.arange(entry_count, dtype=jnp.int32)
    earlier = entry_order[None, :] < entry_order[:, None]
    same_view = source_view[:, :, None] == source_view[:, None, :]
    slot_rank = jnp.sum(jnp.logical_and(same_view, earlier[None]), axis=2)
    slot_index = jnp.arange(capacity, dtype=jnp.int32)
    slot_match = jnp.logical_and(
        (source_view == my_view)[:, :, None], slot_rank[:, :, None] == slot_index[None, None, :]
    )
    strip_table = jnp.sum(jnp.where(slot_match, source_strip[:, :, None], 0), axis=1)
    cross_pairs = projected[:, 4 * head_cols : 6 * head_cols].reshape(
        n_strip, strip_rows, 2 * head_cols
    )
    outgoing = cross_pairs[strip_table]
    received = lax.all_to_all(outgoing, "view", split_axis=0, concat_axis=0, tiled=True)

    def head_block(column_block):
        return projected[:, column_block * head_cols : (column_block + 1) * head_cols].reshape(
            total_rows, heads_here, HEAD_DIM
        )

    self_mix = attend_heads(
        head_block(0), head_block(1), head_block(2), jnp.ones((total_rows,), dtype=bool)
    )
    hidden = projected[:, split_at:]
    my_source = lax.dynamic_index_in_dim(source_view, my_view, 0, keepdims=False)
    my_rank = lax.dynamic_index_in_dim(slot_rank, my_view, 0, keepdims=False)
    picked = received.reshape(n_view * capacity, strip_rows, 2 * head_cols)[
        my_source * capacity + my_rank
    ]
    picked = picked.reshape(n_strip, SLOTS * strip_rows, 2 * head_cols)
    my_count = lax.dynamic_index_in_dim(source_count, my_view, 0, keepdims=False)
    key_valid = jnp.repeat(
        jnp.arange(SLOTS, dtype=jnp.int32)[None, :] < my_count[:, None], strip_rows, axis=1
    )
    cross_heads = projected[:, 3 * head_cols : 4 * head_cols].reshape(
        n_strip, strip_rows, heads_here, HEAD_DIM
    )
    picked_keys = picked[:, :, :head_cols].reshape(
        n_strip, SLOTS * strip_rows, heads_here, HEAD_DIM
    )
    picked_values = picked[:, :, head_cols:].reshape(
        n_strip, SLOTS * strip_rows, heads_here, HEAD_DIM
    )
    cross_mix = jax.vmap(attend_heads)(cross_heads, picked_keys, picked_values, key_valid).reshape(
        total_rows, head_cols
    )
    early_part = lax.psum_scatter(
        (branch_term(self_mix, self_out) + branch_term(hidden, mlp_down)).astype(jnp.bfloat16),
        "strip",
        scatter_dimension=0,
        tiled=True,
    ).astype(jnp.float32)
    cross_part = lax.psum_scatter(
        branch_term(cross_mix, cross_out).astype(jnp.bfloat16),
        "strip",
        scatter_dimension=0,
        tiled=True,
    ).astype(jnp.float32)
    summed = early_part + cross_part
    return (tokens[0].astype(jnp.float32) + summed).astype(jnp.bfloat16)[None]


def solution(mesh):
    in_specs = (
        P("view", "strip", None),
        P(),
        P(),
        P(None, "strip"),
        P(None, "strip"),
        P(None, "strip"),
        P("strip", None),
        P(None, "strip"),
        P(None, "strip"),
        P(None, "strip"),
        P("strip", None),
        P(None, "strip"),
        P("strip", None),
    )
    out_specs = P("view", "strip", None)
    return jax.shard_map(
        per_device, mesh=mesh, in_specs=in_specs, out_specs=out_specs, check_vma=False
    )
```

profile of v0, /device:TPU:12, one launch (start us, length us, event | category | flops | bytes accessed | tf_op | source)
XLA Modules:
  0.0 247.6 jit_solution(7047850341351948367)
XLA Ops:
  13.5 2.2 copy.71
  15.7 2.2 copy.72
  17.9 2.2 copy.73
  20.2 2.2 copy.74
  22.4 2.2 copy.75
  24.6 10.7 %concatenate.5 = bf16[1536,1920]{1,0:T(8,128)(2,1)} concatenate(bf16[1536,192]{1,0:T(8,128)(2,1)S(1)} %copy.70, bf16[1536,192]{1,0:T(8,128)(2,1)} %copy.71, bf16[1536,192]{1,0:T(8,128)(2,1)} %copy.72, bf16[1536,192]{1,0:T(8,128)(2,1)} %copy.73, bf16[1536,192]{1,0:T(8,128)(2,1)} %copy.74, bf16[1536,192]{1,0:T(8,128)(2,1)} %copy.75, bf16[1536,768]{1,0:T(8,128)(2,1)} %param.24), dimensions={1} | concatenate | bytes 11796480 | tf_op jit(solution)/shard_map/concatenate | solution.py:58
  35.9 21.9 %all-gather.2.cloned.1.call-done = bf16[1024,1536]{1,0:T(8,128)(2,1)} async-done(((bf16[128,1536]{1,0:T(8,128)(2,1)}), bf16[1024,1536]{1,0:T(8,128)(2,1)}) %all-gather.2.cloned.1.call-update) | async-done | bytes 3145744 | tf_op jit(solution)/shard_map/all_gather | solution.py:63
  57.7 11.9 %fusion.61 = (bf16[1024,1920]{1,0:T(8,128)(2,1)S(1)}, f32[1024,1920]{1,0:T(8,128)}) fusion(bf16[1024,1536]{1,0:T(8,128)(2,1)} %all-gather.2.cloned.1.call-done, bf16[1536,1920]{1,0:T(8,128)(2,1)} %concatenate.5), kind=kOutput, calls=%fused_computation.87 | convolution fusion | flops 6041763840 | bytes 20840448 | tf_op jit(solution)/shard_map/dot_general | solution.py:62
  74.8 4.1 %gather_fusion = bf16[64,128,384]{2,1,0:T(8,128)(2,1)} fusion(bf16[8,128,384]{2,1,0:T(8,128)(2,1)S(1)} %bitcast.59, s32[1024]{0:T(1024)} %pad_clamp_fusion.1), kind=kCustom, calls=%fused_computation | custom fusion | bytes 12583168 | tf_op jit(solution)/shard_map/gather | solution.py:87
  79.0 7.4 %all-to-all-start = ((bf16[32,2,128,384]{3,2,1,0:T(8,128)(2,1)}), bf16[32,2,128,384]{3,2,1,0:T(8,128)(2,1)}, u32[]{:S(2)}, u32[]{:S(2)}) async-start(bf16[32,2,128,384]{3,2,1,0:T(8,128)(2,1)} %bitcast.60), calls=%async_computation.1 | async-start | bytes 12582912 | tf_op jit(solution)/shard_map/all_to_all | solution.py:88
  86.7 7.7 %fusion.22 = f32[1024,1536]{1,0:T(8,128)} fusion(bf16[768,1536]{1,0:T(8,128)(2,1)S(1)} %copy-done, f32[1024,1920]{1,0:T(8,128)} %get-tuple-element.14), kind=kOutput, calls=%fused_computation.30 | convolution fusion | flops 2422996992 | bytes 11796480 | tf_op jit(solution)/shard_map/dot_general | solution.py:32
  94.4 7.4 %fusion.67 = (f32[3,1024]{1,0:T(4,128)S(1)}, f32[3,1024,1024]{1,2,0:T(8,128)}) fusion(bf16[1024,3,64]{0,2,1:T(8,128)(2,1)S(1)} %bitcast.68, bf16[1024,3,64]{0,2,1:T(8,128)(2,1)S(1)} %bitcast.67), kind=kOutput, calls=%fused_computation.89 | convolution fusion | flops 412091392 | bytes 13381632 | tf_op jit(solution)/shard_map/sub | solution.py:24
  101.9 5.8 %fusion.29 = bf16[3,64,1024]{2,1,0:T(8,128)(2,1)S(1)} fusion(bf16[1024,3,64]{0,2,1:T(8,128)(2,1)S(1)} %bitcast.69, f32[3,1024,1024]{1,2,0:T(8,128)} %get-tuple-element.18, f32[3,1024]{1,0:T(4,128)S(1)} %get-tuple-element.17), kind=kOutput, calls=%fused_computation.36 | convolution fusion | flops 409141248 | bytes 13381632 | tf_op jit(solution)/shard_map/hqk,khe->qhe/dot_general | solution.py:25
  107.8 5.6 %add_convert_fusion = bf16[1024,1536]{1,0:T(8,128)(2,1)} fusion(f32[1024,1536]{1,0:T(8,128)} %fusion.22, bf16[1024,192]{0,1:T(8,128)(2,1)S(1)} %bitcast.66, bf16[192,1536]{1,0:T(8,128)(2,1)S(1)} %copy-done.5), kind=kOutput, calls=%fused_computation.11 | convolution fusion | flops 607125504 | bytes 10420224 | tf_op jit(solution)/shard_map/dot_general | solution.py:32
  115.0 44.2 %all-to-all-done = bf16[32,2,128,384]{3,2,1,0:T(8,128)(2,1)} async-done(((bf16[32,2,128,384]{3,2,1,0:T(8,128)(2,1)}), bf16[32,2,128,384]{3,2,1,0:T(8,128)(2,1)}, u32[]{:S(2)}, u32[]{:S(2)}) %all-to-all-start) | async-done | bytes 6291488 | tf_op jit(solution)/shard_map/all_to_all | solution.py:88
  159.2 6.1 %gather_fusion.1 = bf16[40,128,384]{2,1,0:T(8,128)(2,1)} fusion(bf16[64,128,384]{2,1,0:T(8,128)(2,1)} %bitcast.10, s32[1024]{0:T(1024)S(1)} %pad_clamp_fusion), kind=kCustom, calls=%fused_computation.1 | custom fusion | bytes 7864480 | tf_op jit(solution)/shard_map/gather | solution.py:101
  165.3 6.4 %fusion.60 = (bf16[8,640,192]{2,1,0:T(8,128)(2,1)}, bf16[8,640,192]{2,1,0:T(8,128)(2,1)}) fusion(bf16[8,640,384]{2,1,0:T(8,128)(2,1)} %bitcast.61), kind=kLoop, calls=%fused_computation.86 | loop fusion | bytes 7864320 | tf_op jit(solution)/shard_map/slice | solution.py:112
  171.6 3.0 %copy.88 = bf16[8,640,192]{1,2,0:T(8,128)(2,1)S(1)} copy(bf16[8,640,192]{2,1,0:T(8,128)(2,1)} %get-tuple-element.11) | data formatting | bytes 3932160 | tf_op jit(solution)/shard_map/slice | solution.py:112
  174.7 4.3 %copy.86 = bf16[8,640,192]{1,2,0:T(8,128)(2,1)} copy(bf16[8,640,192]{2,1,0:T(8,128)(2,1)} %get-tuple-element.12) | data formatting | bytes 3932160 | tf_op jit(solution)/shard_map/slice | solution.py:115
  179.0 4.8 %fusion.62 = (f32[8,3,128]{2,1,0:T(4,128)S(1)}, f32[8,3,128,640]{3,2,1,0:T(8,128)}) fusion(pred[8,640]{1,0:T(8,128)(4,1)S(1)} %broadcast_bitcast_fusion, bf16[8,640,3,64]{1,3,2,0:T(8,128)(2,1)S(1)} %bitcast.63, bf16[8,128,3,64]{1,0,3,2:T(8,128)(2,1)S(1)} %bitcast.70), kind=kOutput, calls=%fused_computation.88 | convolution fusion | flops 259523200 | bytes 10241024 | tf_op jit(solution)/shard_map/vmap()/sub | solution.py:24
  183.8 5.6 %fusion.30 = bf16[8,128,3,64]{1,3,2,0:T(8,128)(2,1)S(1)} fusion(bf16[8,640,3,64]{1,3,2,0:T(8,128)(2,1)} %bitcast.64, f32[8,3,128,640]{3,2,1,0:T(8,128)} %get-tuple-element.16, f32[8,3,128]{2,1,0:T(4,128)S(1)} %get-tuple-element.15), kind=kOutput, calls=%fused_computation.37 | convolution fusion | flops 255787008 | bytes 10235904 | tf_op jit(solution)/shard_map/vmap(hqk,khe->qhe)/dot_general | solution.py:25
  189.7 2.7 %convolution_convert_fusion = bf16[1024,1536]{1,0:T(8,128)(2,1)} fusion(bf16[192,1536]{1,0:T(8,128)(2,1)S(1)} %copy-done.6, bf16[24,8,8,128]{3,2,1,0:T(8,128)(2,1)S(1)} %bitcast.62), kind=kOutput, calls=%fused_computation.21 | convolution fusion | flops 605552640 | bytes 4128768 | tf_op jit(solution)/shard_map/dot_general | solution.py:32
  192.4 46.6 %reduce-scatter.5.cloned.1.call-done = bf16[128,1536]{1,0:T(8,128)(2,1)} async-done(((bf16[1024,1536]{1,0:T(8,128)(2,1)}), bf16[128,1536]{1,0:T(8,128)(2,1)}) %reduce-scatter.5.cloned.1.call-update) | async-done | bytes 393232 | tf_op jit(solution)/shard_map/reduce_scatter | solution.py:127
  239.0 2.0 fusion.36
  (56 shorter events, 14.9 us)
Async XLA Ops:
  6.5 80.1 %copy-start = (bf16[768,1536]{1,0:T(8,128)(2,1)S(1)}, bf16[768,1536]{1,0:T(8,128)(2,1)}, u32[]{:S(2)}) copy-start(bf16[768,1536]{1,0:T(8,128)(2,1)} %param.25) | copy-start | bytes 7077892
  6.5 51.2 %all-gather.2.cloned.1.call-start = ((), (), s32[]{:S(2)}) async-start(), calls=%async_computation.3 | async-start | bytes 3538944 | tf_op jit(solution)/shard_map/all_gather | solution.py:63
  11.4 0.6 copy-start.8
  79.0 80.2 %all-to-all-start = ((bf16[32,2,128,384]{3,2,1,0:T(8,128)(2,1)}), bf16[32,2,128,384]{3,2,1,0:T(8,128)(2,1)}, u32[]{:S(2)}, u32[]{:S(2)}) async-start(bf16[32,2,128,384]{3,2,1,0:T(8,128)(2,1)} %bitcast.60), calls=%async_computation.1 | async-start | bytes 12582912 | tf_op jit(solution)/shard_map/all_to_all | solution.py:88
  86.4 106.0 %reduce-scatter.3.cloned.1.call-start = ((), (), s32[]{:S(2)}) async-start(), calls=%async_computation.4 | async-start | bytes 3538944 | tf_op jit(solution)/shard_map/reduce_scatter | solution.py:121
  86.7 7.7 %copy-start.7 = (bf16[1024,192]{0,1:T(8,128)(2,1)S(1)}, bf16[1024,192]{0,1:T(8,128)(2,1)}, u32[]{:S(2)}) copy-start(bf16[1024,192]{0,1:T(8,128)(2,1)} %copy.77) | copy-start | bytes 1179652
  94.4 7.4 %copy-start.4 = (bf16[1024,192]{1,0:T(8,128)(2,1)S(1)}, bf16[1024,192]{1,0:T(8,128)(2,1)}, u32[]{:S(2)}) copy-start(bf16[1024,192]{1,0:T(8,128)(2,1)} %get-tuple-element.10) | copy-start | bytes 1179652
  101.9 5.9 %copy-start.5 = (bf16[192,1536]{1,0:T(8,128)(2,1)S(1)}, bf16[192,1536]{1,0:T(8,128)(2,1)}, u32[]{:S(2)}) copy-start(bf16[192,1536]{1,0:T(8,128)(2,1)} %param.19) | copy-start | bytes 1769476
  107.8 5.9 %copy-start.9 = (s32[32,8]{0,1:T(8,128)S(1)}, s32[32,8]{0,1:T(8,128)}, u32[]{:S(2)}) copy-start(s32[32,8]{0,1:T(8,128)} %param.15) | copy-start | bytes 3076
  107.8 6.9 %copy-start.3 = (bf16[1024,192]{1,0:T(8,128)(2,1)S(1)}, bf16[1024,192]{1,0:T(8,128)(2,1)}, u32[]{:S(2)}) copy-start(bf16[1024,192]{1,0:T(8,128)(2,1)} %get-tuple-element.8) | copy-start | bytes 1179652
  113.4 125.6 %reduce-scatter.5.cloned.1.call-start = ((), (), s32[]{:S(2)}) async-start(), calls=%async_computation.5 | async-start | bytes 3538944 | tf_op jit(solution)/shard_map/reduce_scatter | solution.py:127
  183.8 5.9 %copy-start.6 = (bf16[192,1536]{1,0:T(8,128)(2,1)S(1)}, bf16[192,1536]{1,0:T(8,128)(2,1)}, u32[]{:S(2)}) copy-start(bf16[192,1536]{1,0:T(8,128)(2,1)} %param.23) | copy-start | bytes 1769476
  189.7 49.4 %copy-start.2 = (bf16[1,128,1536]{2,1,0:T(8,128)(2,1)S(1)}, bf16[1,128,1536]{2,1,0:T(8,128)(2,1)}, u32[]{:S(2)}) copy-start(bf16[1,128,1536]{2,1,0:T(8,128)(2,1)} %param.13) | copy-start | bytes 1179652
  189.7 51.4 %copy-start.1 = (bf16[768,1536]{1,0:T(8,128)(2,1)S(1)}, bf16[768,1536]{1,0:T(8,128)(2,1)}, u32[]{:S(2)}) copy-start(bf16[768,1536]{1,0:T(8,128)(2,1)} %param.25) | copy-start | bytes 7077892
Sparse Core Ops, SparseCore 0:
  9.9 47.8 all-gather.1
  113.6 45.5 reduce-scatter.2
  192.5 46.4 reduce-scatter.4
where the time goes:
time: 249 us; the launch traced here: 248 us
  waiting for transfers between devices  113 us (45%)
  local copies, waits for them, and re-layouts  54.6 us (22%)
  matrix products  51.5 us (21%)
  between operations  13.3 us (5%)
  starting transfers between devices  7.93 us (3%)
  other arithmetic  7.46 us (3%)
    reduce_scatter x1, waiting for transfers between devices, per_device(): lax.psum_scatter(branch_term(cross_mix, cross_out).astype(jnp.bfloat16),...  46.6 us
    all_to_all x1, waiting for transfers between devices, per_device(): lax.all_to_all(outgoing, 'view', split_axis=0, concat_axis=0, tiled=True)  44.2 us
    all_gather x1, waiting for transfers between devices, per_device(): lax.all_gather(normed, 'strip', axis=0, tiled=True)  21.9 us
    dot_general x3, matrix products, branch_term(): return jnp.dot(mixed_rows, weight, preferred_element_type=jnp.float32)  16 us
    unnamed x28, local copies, waits for them, and re-layouts  13.7 us
    sub x2, matrix products, attend_heads(): weights = jax.nn.softmax(scores, axis=-1).astype(jnp.bfloat16)  12.1 us
    dot_general x1, matrix products, per_device(): jnp.dot(lax.all_gather(normed, 'strip', axis=0, tiled=True), stacked, pre...  11.9 us
    dot_general x2, matrix products, attend_heads(): jnp.einsum('hqk,khe->qhe', weights, value_heads, preferred_element_type=j...  11.4 us
  transfers between devices with their start and end apart: 4, of which 3 were waited for; matrix products, arithmetic and copies ran while one was open for 35% of the time, Pallas kernels for 0%

commit v1 on v0

--- a/solution.py
+++ b/solution.py
@@ -60,7 +60,9 @@
     )
     split_at = 6 * head_cols
     product = jnp.dot(
-        lax.all_gather(normed, "strip", axis=0, tiled=True),
+        jnp.concatenate(
+            lax.all_to_all(jnp.stack([normed] * lax.axis_size("strip")), "strip", 0, 0), axis=0
+        ),
         stacked,
         preferred_element_type=jnp.float32,
     )

time: 249 us -> 282 us (1.13)
  waiting for transfers between devices: 113 us -> 137 us
  starting transfers between devices: 7.93 us -> 16.6 us
    all_to_all x0 -> x1, waiting for transfers between devices: none -> 48.5 us  [per_device(): lax.all_to_all(jnp.stack([normed] * lax.axis_size('strip')), 'strip', 0, 0)]
    all_gather x1 -> x0, waiting for transfers between devices: 21.9 us -> none  [per_device(): lax.all_gather(normed, 'strip', axis=0, tiled=True)]
    all_to_all x0 -> x1, starting transfers between devices: none -> 8.6 us  [per_device(): lax.all_to_all(jnp.stack([normed] * lax.axis_size('strip')), 'strip', 0, 0)]
    unnamed x28 -> x30, local copies, waits for them, and re-layouts: 13.7 us -> 13 us
  transfers between devices with their start and end apart: 4 -> 4, of which waited for: 3 -> 3; matrix products, arithmetic and copies ran while one was open for 35% -> 31% of each run, Pallas kernels for 0% -> 0%
where the time goes in v1:
time: 282 us; the launch traced here: 281 us
  waiting for transfers between devices  137 us (49%)
  local copies, waits for them, and re-layouts  55.8 us (20%)
  matrix products  51.5 us (18%)
  starting transfers between devices  16.6 us (6%)
  between operations  13.6 us (5%)
  other arithmetic  6.72 us (2%)
    all_to_all x1, waiting for transfers between devices, per_device(): lax.all_to_all(jnp.stack([normed] * lax.axis_size('strip')), 'strip', 0, 0)  48.5 us
    all_to_all x1, waiting for transfers between devices, per_device(): lax.all_to_all(outgoing, 'view', split_axis=0, concat_axis=0, tiled=True)  44.2 us
    reduce_scatter x1, waiting for transfers between devices, per_device(): lax.psum_scatter(branch_term(cross_mix, cross_out).astype(jnp.bfloat16),...  44 us
    dot_general x3, matrix products, branch_term(): return jnp.dot(mixed_rows, weight, preferred_element_type=jnp.float32)  16 us
    unnamed x30, local copies, waits for them, and re-layouts  13 us
    sub x2, matrix products, attend_heads(): weights = jax.nn.softmax(scores, axis=-1).astype(jnp.bfloat16)  12.1 us
    dot_general x1, matrix products, per_device(): jnp.dot(jnp.concatenate(lax.all_to_all(jnp.stack([normed] * lax.axis_size...  11.9 us
    dot_general x2, matrix products, attend_heads(): jnp.einsum('hqk,khe->qhe', weights, value_heads, preferred_element_type=j...  11.4 us
  transfers between devices with their start and end apart: 4, of which 3 were waited for; matrix products, arithmetic and copies ran while one was open for 31% of the time, Pallas kernels for 0%

profile of v1, /device:TPU:12, one launch (start us, length us, event | category | flops | bytes accessed | tf_op | source)
XLA Modules:
  0.0 281.1 jit_solution(16683540514891628597)
XLA Ops:
  10.9 8.6 %all-to-all-start = ((bf16[8,128,1536]{2,1,0:T(8,128)(2,1)}), bf16[8,128,1536]{2,1,0:T(8,128)(2,1)}, u32[]{:S(2)}, u32[]{:S(2)}) async-start(bf16[8,128,1536]{2,1,0:T(8,128)(2,1)} %stack.5), calls=%async_computation | async-start | bytes 6291456 | tf_op jit(solution)/shard_map/all_to_all | solution.py:64
  22.5 2.2 copy.71
  24.7 2.2 copy.72
  27.0 2.2 copy.73
  29.2 2.3 copy.74
  31.5 2.2 copy.75
  33.7 10.6 %concatenate.5 = bf16[1536,1920]{1,0:T(8,128)(2,1)} concatenate(bf16[1536,192]{1,0:T(8,128)(2,1)S(1)} %copy.70, bf16[1536,192]{1,0:T(8,128)(2,1)} %copy.71, bf16[1536,192]{1,0:T(8,128)(2,1)} %copy.72, bf16[1536,192]{1,0:T(8,128)(2,1)} %copy.73, bf16[1536,192]{1,0:T(8,128)(2,1)} %copy.74, bf16[1536,192]{1,0:T(8,128)(2,1)} %copy.75, bf16[1536,768]{1,0:T(8,128)(2,1)} %param.24), dimensions={1} | concatenate | bytes 11796480 | tf_op jit(solution)/shard_map/concatenate | solution.py:58
  44.9 48.5 %all-to-all-done = bf16[8,128,1536]{2,1,0:T(8,128)(2,1)} async-done(((bf16[8,128,1536]{2,1,0:T(8,128)(2,1)}), bf16[8,128,1536]{2,1,0:T(8,128)(2,1)}, u32[]{:S(2)}, u32[]{:S(2)}) %all-to-all-start) | async-done | bytes 3145760 | tf_op jit(solution)/shard_map/all_to_all | solution.py:64
  93.4 11.9 %fusion.64 = (bf16[1024,1920]{1,0:T(8,128)(2,1)S(1)}, f32[1024,1920]{1,0:T(8,128)}) fusion(bf16[1024,1536]{1,0:T(8,128)(2,1)} %bitcast.2, bf16[1536,1920]{1,0:T(8,128)(2,1)} %concatenate.5), kind=kOutput, calls=%fused_computation.89 | convolution fusion | flops 6041763840 | bytes 20840448 | tf_op jit(solution)/shard_map/dot_general | solution.py:62
  110.5 4.1 %gather_fusion = bf16[64,128,384]{2,1,0:T(8,128)(2,1)} fusion(bf16[8,128,384]{2,1,0:T(8,128)(2,1)S(1)} %bitcast.69, s32[1024]{0:T(1024)} %pad_clamp_fusion.1), kind=kCustom, calls=%fused_computation | custom fusion | bytes 12583168 | tf_op jit(solution)/shard_map/gather | solution.py:89
  114.6 7.5 %all-to-all-start.1 = ((bf16[32,2,128,384]{3,2,1,0:T(8,128)(2,1)}), bf16[32,2,128,384]{3,2,1,0:T(8,128)(2,1)}, u32[]{:S(2)}, u32[]{:S(2)}) async-start(bf16[32,2,128,384]{3,2,1,0:T(8,128)(2,1)} %bitcast.70), calls=%async_computation.2 | async-start | bytes 12582912 | tf_op jit(solution)/shard_map/all_to_all | solution.py:90
  122.4 7.7 %fusion.22 = f32[1024,1536]{1,0:T(8,128)} fusion(bf16[768,1536]{1,0:T(8,128)(2,1)S(1)} %copy-done, f32[1024,1920]{1,0:T(8,128)} %get-tuple-element.14), kind=kOutput, calls=%fused_computation.30 | convolution fusion | flops 2422996992 | bytes 11796480 | tf_op jit(solution)/shard_map/dot_general | solution.py:32
  130.1 7.4 %fusion.70 = (f32[3,1024]{1,0:T(4,128)S(1)}, f32[3,1024,1024]{1,2,0:T(8,128)}) fusion(bf16[1024,3,64]{0,2,1:T(8,128)(2,1)S(1)} %bitcast.78, bf16[1024,3,64]{0,2,1:T(8,128)(2,1)S(1)} %bitcast.77), kind=kOutput, calls=%fused_computation.91 | convolution fusion | flops 412091392 | bytes 13381632 | tf_op jit(solution)/shard_map/sub | solution.py:24
  137.7 5.8 %fusion.29 = bf16[3,64,1024]{2,1,0:T(8,128)(2,1)S(1)} fusion(bf16[1024,3,64]{0,2,1:T(8,128)(2,1)S(1)} %bitcast.79, f32[3,1024,1024]{1,2,0:T(8,128)} %get-tuple-element.18, f32[3,1024]{1,0:T(4,128)S(1)} %get-tuple-element.17), kind=kOutput, calls=%fused_computation.36 | convolution fusion | flops 409141248 | bytes 13381632 | tf_op jit(solution)/shard_map/hqk,khe->qhe/dot_general | solution.py:25
  143.6 5.6 %add_convert_fusion = bf16[1024,1536]{1,0:T(8,128)(2,1)} fusion(f32[1024,1536]{1,0:T(8,128)} %fusion.22, bf16[1024,192]{0,1:T(8,128)(2,1)S(1)} %bitcast.76, bf16[192,1536]{1,0:T(8,128)(2,1)S(1)} %copy-done.5), kind=kOutput, calls=%fused_computation.11 | convolution fusion | flops 607125504 | bytes 10420224 | tf_op jit(solution)/shard_map/dot_general | solution.py:32
  150.7 44.2 %all-to-all-done.1 = bf16[32,2,128,384]{3,2,1,0:T(8,128)(2,1)} async-done(((bf16[32,2,128,384]{3,2,1,0:T(8,128)(2,1)}), bf16[32,2,128,384]{3,2,1,0:T(8,128)(2,1)}, u32[]{:S(2)}, u32[]{:S(2)}) %all-to-all-start.1) | async-done | bytes 6291488 | tf_op jit(solution)/shard_map/all_to_all | solution.py:90
  195.0 6.1 %gather_fusion.1 = bf16[40,128,384]{2,1,0:T(8,128)(2,1)} fusion(bf16[64,128,384]{2,1,0:T(8,128)(2,1)} %bitcast.11, s32[1024]{0:T(1024)S(1)} %pad_clamp_fusion), kind=kCustom, calls=%fused_computation.1 | custom fusion | bytes 7864480 | tf_op jit(solution)/shard_map/gather | solution.py:103
  201.0 6.4 %fusion.63 = (bf16[8,640,192]{2,1,0:T(8,128)(2,1)}, bf16[8,640,192]{2,1,0:T(8,128)(2,1)}) fusion(bf16[8,640,384]{2,1,0:T(8,128)(2,1)} %bitcast.71), kind=kLoop, calls=%fused_computation.88 | loop fusion | bytes 7864320 | tf_op jit(solution)/shard_map/slice | solution.py:114
  207.4 3.0 %copy.88 = bf16[8,640,192]{1,2,0:T(8,128)(2,1)S(1)} copy(bf16[8,640,192]{2,1,0:T(8,128)(2,1)} %get-tuple-element.11) | data formatting | bytes 3932160 | tf_op jit(solution)/shard_map/slice | solution.py:114
  210.5 4.3 %copy.86 = bf16[8,640,192]{1,2,0:T(8,128)(2,1)} copy(bf16[8,640,192]{2,1,0:T(8,128)(2,1)} %get-tuple-element.12) | data formatting | bytes 3932160 | tf_op jit(solution)/shard_map/slice | solution.py:117
  214.7 4.8 %fusion.65 = (f32[8,3,128]{2,1,0:T(4,128)S(1)}, f32[8,3,128,640]{3,2,1,0:T(8,128)}) fusion(pred[8,640]{1,0:T(8,128)(4,1)S(1)} %broadcast_bitcast_fusion, bf16[8,640,3,64]{1,3,2,0:T(8,128)(2,1)S(1)} %bitcast.73, bf16[8,128,3,64]{1,0,3,2:T(8,128)(2,1)S(1)} %bitcast.80), kind=kOutput, calls=%fused_computation.90 | convolution fusion | flops 259523200 | bytes 10241024 | tf_op jit(solution)/shard_map/vmap()/sub | solution.py:24
  219.5 5.6 %fusion.30 = bf16[8,128,3,64]{1,3,2,0:T(8,128)(2,1)S(1)} fusion(bf16[8,640,3,64]{1,3,2,0:T(8,128)(2,1)} %bitcast.74, f32[8,3,128,640]{3,2,1,0:T(8,128)} %get-tuple-element.16, f32[8,3,128]{2,1,0:T(4,128)S(1)} %get-tuple-element.15), kind=kOutput, calls=%fused_computation.37 | convolution fusion | flops 255787008 | bytes 10235904 | tf_op jit(solution)/shard_map/vmap(hqk,khe->qhe)/dot_general | solution.py:25
  225.4 2.7 convolution_convert_fusion
  228.2 44.0 %reduce-scatter.5.cloned.1.call-done = bf16[128,1536]{1,0:T(8,128)(2,1)} async-done(((bf16[1024,1536]{1,0:T(8,128)(2,1)}), bf16[128,1536]{1,0:T(8,128)(2,1)}) %reduce-scatter.5.cloned.1.call-update) | async-done | bytes 393232 | tf_op jit(solution)/shard_map/reduce_scatter | solution.py:129
  (58 shorter events, 17.4 us)
Async XLA Ops:
  6.5 115.9 %copy-start = (bf16[768,1536]{1,0:T(8,128)(2,1)S(1)}, bf16[768,1536]{1,0:T(8,128)(2,1)}, u32[]{:S(2)}) copy-start(bf16[768,1536]{1,0:T(8,128)(2,1)} %param.25) | copy-start | bytes 7077892
  10.9 8.6 %copy-start.9 = (s32[32,8,5]{0,1,2:T(8,128)S(1)}, s32[32,8,5]{0,1,2:T(8,128)}, u32[]{:S(2)}) copy-start(s32[32,8,5]{0,1,2:T(8,128)} %param.14) | copy-start | bytes 15364
  10.9 82.5 %all-to-all-start = ((bf16[8,128,1536]{2,1,0:T(8,128)(2,1)}), bf16[8,128,1536]{2,1,0:T(8,128)(2,1)}, u32[]{:S(2)}, u32[]{:S(2)}) async-start(bf16[8,128,1536]{2,1,0:T(8,128)(2,1)} %stack.5), calls=%async_computation | async-start | bytes 6291456 | tf_op jit(solution)/shard_map/all_to_all | solution.py:64
  20.5 0.6 copy-start.8
  114.6 80.3 %all-to-all-start.1 = ((bf16[32,2,128,384]{3,2,1,0:T(8,128)(2,1)}), bf16[32,2,128,384]{3,2,1,0:T(8,128)(2,1)}, u32[]{:S(2)}, u32[]{:S(2)}) async-start(bf16[32,2,128,384]{3,2,1,0:T(8,128)(2,1)} %bitcast.70), calls=%async_computation.2 | async-start | bytes 12582912 | tf_op jit(solution)/shard_map/all_to_all | solution.py:90
  122.2 106.0 %reduce-scatter.3.cloned.1.call-start = ((), (), s32[]{:S(2)}) async-start(), calls=%async_computation.4 | async-start | bytes 3538944 | tf_op jit(solution)/shard_map/reduce_scatter | solution.py:123
  122.4 7.7 %copy-start.7 = (bf16[1024,192]{0,1:T(8,128)(2,1)S(1)}, bf16[1024,192]{0,1:T(8,128)(2,1)}, u32[]{:S(2)}) copy-start(bf16[1024,192]{0,1:T(8,128)(2,1)} %copy.77) | copy-start | bytes 1179652
  130.1 7.4 %copy-start.4 = (bf16[1024,192]{1,0:T(8,128)(2,1)S(1)}, bf16[1024,192]{1,0:T(8,128)(2,1)}, u32[]{:S(2)}) copy-start(bf16[1024,192]{1,0:T(8,128)(2,1)} %get-tuple-element.10) | copy-start | bytes 1179652
  137.7 5.9 %copy-start.5 = (bf16[192,1536]{1,0:T(8,128)(2,1)S(1)}, bf16[192,1536]{1,0:T(8,128)(2,1)}, u32[]{:S(2)}) copy-start(bf16[192,1536]{1,0:T(8,128)(2,1)} %param.19) | copy-start | bytes 1769476
  143.6 5.9 %copy-start.10 = (s32[32,8]{0,1:T(8,128)S(1)}, s32[32,8]{0,1:T(8,128)}, u32[]{:S(2)}) copy-start(s32[32,8]{0,1:T(8,128)} %param.15) | copy-start | bytes 3076
  143.6 6.9 %copy-start.3 = (bf16[1024,192]{1,0:T(8,128)(2,1)S(1)}, bf16[1024,192]{1,0:T(8,128)(2,1)}, u32[]{:S(2)}) copy-start(bf16[1024,192]{1,0:T(8,128)(2,1)} %get-tuple-element.8) | copy-start | bytes 1179652
  149.2 123.0 %reduce-scatter.5.cloned.1.call-start = ((), (), s32[]{:S(2)}) async-start(), calls=%async_computation.5 | async-start | bytes 3538944 | tf_op jit(solution)/shard_map/reduce_scatter | solution.py:129
  219.5 5.9 %copy-start.6 = (bf16[192,1536]{1,0:T(8,128)(2,1)S(1)}, bf16[192,1536]{1,0:T(8,128)(2,1)}, u32[]{:S(2)}) copy-start(bf16[192,1536]{1,0:T(8,128)(2,1)} %param.23) | copy-start | bytes 1769476
  225.4 46.8 %copy-start.2 = (bf16[1,128,1536]{2,1,0:T(8,128)(2,1)S(1)}, bf16[1,128,1536]{2,1,0:T(8,128)(2,1)}, u32[]{:S(2)}) copy-start(bf16[1,128,1536]{2,1,0:T(8,128)(2,1)} %param.13) | copy-start | bytes 1179652
  225.4 48.8 %copy-start.1 = (bf16[768,1536]{1,0:T(8,128)(2,1)S(1)}, bf16[768,1536]{1,0:T(8,128)(2,1)}, u32[]{:S(2)}) copy-start(bf16[768,1536]{1,0:T(8,128)(2,1)} %param.25) | copy-start | bytes 7077892
Sparse Core Ops, SparseCore 0:
  149.3 43.2 reduce-scatter.2
  228.3 43.9 reduce-scatter.4
